TPU v7x, 512 devices: a whole 4x4x16 slice. The times are simulated.
512 devices in a mesh: blk: 8 (over y, core), tiles: 64 (over z, x).
Axes of the slice: x: 4, y: 4, z: 16, core: 2. Of those that a mesh axis runs over, the one named last changes fastest.
Arguments:
- tensor_tiles: bfloat16 [8, 128, 64, 4096], P('blk', 'tiles'), may hold values from -6 to 6
- tile_iblock: int32 [8, 128], P('blk', 'tiles'), may hold values from 0 to 7
- tile_jslot: int32 [8, 128], P('blk', 'tiles'), may hold values from 0 to 1, as said below
- tile_kslot: int32 [8, 128], P('blk', 'tiles'), may hold values from 0 to 1, as said below
- block_jlist: int32 [8, 128], P('blk', 'tiles'), may hold values from 0 to 255, as said below
- block_klist: int32 [8, 128], P('blk', 'tiles'), may hold values from 0 to 63, as said below
- factor_b: bfloat16 [256, 64, 512], P(None, 'tiles'), may hold values from -0.5 to 0.5
- factor_c: bfloat16 [64, 64, 512], P(None, 'tiles'), may hold values from -0.75 to 0.75
Outputs:
- mttkrp: float32 [32768, 512], P(('blk', 'tiles'))
Inputs may be any that keep to these rules, and one draw needn't show every extreme that they name: `block_jlist`: the 2 entries of one device's list are distinct. `block_klist`: the 2 entries of one device's list are distinct. `tile_jslot`: one device's tiles use between 1 and 2 distinct positions, and all 2 on some device. `tile_kslot`: one device's tiles use between 1 and 2 distinct positions, and all 2 on some device.
All inputs are finite; a program needn't handle non-finite values.
Results may differ from a plain program's by a relative error of at most 0.011.
Values may be sent and summed in bfloat16 or wider, within the bound.
A program may use at most 64 MiB of HBM per device.

v0:
```python
import jax
import jax.numpy as jnp
from jax import lax
from jax.sharding import PartitionSpec as P


def outgoing(asked, local, width):
    peers = asked.shape[0] // width
    table = asked.reshape(peers, width).T
    return jnp.take(local, table, axis=0)


def tile_term(local_tiles, which, mode_two, mode_three):
    tile_block = lax.dynamic_index_in_dim(local_tiles, which, 0, keepdims=False)
    inner = tile_block.shape[0]
    across = mode_two.shape[0]
    depth = mode_three.shape[0]
    contracted = jnp.dot(
        tile_block.reshape(inner * across, depth), mode_three, preferred_element_type=jnp.float32
    )
    return jnp.sum(
        contracted.reshape(inner, across, -1) * mode_two.astype(jnp.float32)[None], axis=1
    )


def per_device(
    tensor_tiles, tile_iblock, tile_jslot, tile_kslot, block_jlist, block_klist, factor_b, factor_c
):
    local_tiles = tensor_tiles[0]
    slots_two = tile_jslot[0]
    slots_three = tile_kslot[0]
    count = local_tiles.shape[0]
    wanted_two = jnp.take(block_jlist[0], slots_two)
    wanted_three = jnp.take(block_klist[0], slots_three)
    asked_two, asked_three = (
        lax.all_gather(wanted_two, "tiles", axis=0, tiled=True),
        lax.all_gather(wanted_three, "tiles", axis=0, tiled=True),
    )
    recv_two, recv_three = (
        lax.all_to_all(
            outgoing(asked_two, factor_b, count), "tiles", split_axis=1, concat_axis=2, tiled=True
        ),
        lax.all_to_all(
            outgoing(asked_three, factor_c, count), "tiles", split_axis=1, concat_axis=2, tiled=True
        ),
    )
    pick_two = jnp.arange(count, dtype=jnp.int32)
    pick_three = jnp.arange(count, dtype=jnp.int32)
    rank = factor_b.shape[2]
    fetched_two = recv_two.reshape(count, -1, rank)
    fetched_three = recv_three.reshape(count, -1, rank)
    groups = lax.axis_size("blk")
    inner = local_tiles.shape[1]
    owners = tile_iblock[0]

    def accumulate(which, partial_value):
        mode_two = lax.dynamic_index_in_dim(fetched_two, pick_two[which], 0, keepdims=False)
        mode_three = lax.dynamic_index_in_dim(fetched_three, pick_three[which], 0, keepdims=False)
        term = tile_term(local_tiles, which, mode_two, mode_three)
        target = owners[which]
        current = lax.dynamic_index_in_dim(partial_value, target, 0, keepdims=False)
        return lax.dynamic_update_index_in_dim(partial_value, current + term, target, 0)

    partial_value = lax.fori_loop(
        0, count, accumulate, jnp.zeros((groups, inner, rank), jnp.float32)
    )
    rounded = lax.optimization_barrier(partial_value.astype(jnp.bfloat16)).astype(jnp.float32)
    return lax.psum_scatter(
        rounded.reshape(groups * inner, rank).astype(jnp.bfloat16),
        "blk",
        scatter_dimension=0,
        tiled=True,
    ).astype(jnp.float32)


def solution(mesh):
    placed = (
        P("blk", "tiles", None, None),
        P("blk", "tiles"),
        P("blk", "tiles"),
        P("blk", "tiles"),
        P("blk", "tiles"),
        P("blk", "tiles"),
        P(None, "tiles", None),
        P(None, "tiles", None),
    )
    return jax.shard_map(
        per_device, mesh=mesh, in_specs=placed, out_specs=P(("blk", "tiles"), None), check_vma=False
    )
```

profile of v0, /device:TPU:4, one launch (start us, length us, event | category | flops | bytes accessed | tf_op | source)
XLA Modules:
  0.0 147.8 jit_solution(16779231108427683180)
XLA Ops:
  6.5 0.0 copy-start
  6.5 0.0 copy-start.2
  6.5 0.0 copy-start.3
  6.5 0.0 copy-start.1
  6.5 0.7 compare_select_fusion.3
  7.3 0.7 compare_select_fusion.2
  7.9 1.3 dynamic-slice
  9.9 1.3 gather_fusion.2
  11.2 1.3 gather_fusion.3
  12.5 0.0 copy-done.2
  12.5 0.1 fusion.4
  12.5 0.0 copy-done.3
  12.5 0.1 fusion.5
  12.6 31.5 %all-reduce.2 = (s32[128]{0:T(128)S(1)}, s32[128]{0:T(128)S(1)}) all-reduce(s32[128]{0:T(128)S(1)} %fusion.4, s32[128]{0:T(128)S(1)} %fusion.5), channel_id=1, replica_groups=mesh['blk'=8,'tiles'=64] {'tiles'}, use_global_device_ids=true, to_apply=%add | all-reduce | flops 256 | bytes 2048
  44.1 0.1 reshape.69
  44.3 0.1 copy.17
  44.3 0.1 reshape.94
  44.4 0.0 copy-done.1
  44.4 0.9 gather_fusion
  45.3 0.9 broadcast_select_fusion.1
  46.2 10.3 %all-to-all-start = ((bf16[2,64,1,512]{3,0,2,1:T(2,128)(2,1)}), bf16[2,64,1,512]{3,0,2,1:T(2,128)(2,1)S(1)}, u32[]{:S(2)}, u32[]{:S(2)}) async-start(bf16[2,64,1,512]{3,0,2,1:T(2,128)(2,1)} %broadcast_select_fusion.1), calls=%async_computation | async-start | bytes 262144 | tf_op jit(solution)/shard_map/all_to_all | solution.py:43
  56.5 0.1 reshape.71
  56.6 0.1 copy.19
  56.7 0.1 reshape.104
  56.8 0.0 copy-done
  56.8 0.9 gather_fusion.1
  57.7 0.0 copy-start.4
  57.7 0.9 broadcast_select_fusion
  58.6 12.3 %all-to-all-done = bf16[2,64,1,512]{3,0,2,1:T(2,128)(2,1)S(1)} async-done(((bf16[2,64,1,512]{3,0,2,1:T(2,128)(2,1)}), bf16[2,64,1,512]{3,0,2,1:T(2,128)(2,1)S(1)}, u32[]{:S(2)}, u32[]{:S(2)}) %all-to-all-start) | async-done | bytes 131104 | tf_op jit(solution)/shard_map/all_to_all | solution.py:43
  70.8 6.3 %all-to-all-start.1 = ((bf16[2,64,1,512]{3,0,2,1:T(2,128)(2,1)}), bf16[2,64,1,512]{3,0,2,1:T(2,128)(2,1)S(1)}, u32[]{:S(2)}, u32[]{:S(2)}) async-start(bf16[2,64,1,512]{3,0,2,1:T(2,128)(2,1)} %broadcast_select_fusion), calls=%async_computation.1 | async-start | bytes 262144 | tf_op jit(solution)/shard_map/all_to_all | solution.py:40
  77.2 0.0 reduce-scatter.2.cloned.1.call-start
  77.2 14.5 %all-to-all-done.1 = bf16[2,64,1,512]{3,0,2,1:T(2,128)(2,1)S(1)} async-done(((bf16[2,64,1,512]{3,0,2,1:T(2,128)(2,1)}), bf16[2,64,1,512]{3,0,2,1:T(2,128)(2,1)S(1)}, u32[]{:S(2)}, u32[]{:S(2)}) %all-to-all-start.1) | async-done | bytes 131104 | tf_op jit(solution)/shard_map/all_to_all | solution.py:40
  91.7 0.1 broadcast_in_dim.33
  91.9 0.0 copy-done.4
  91.9 16.1 %while.14 = (s32[]{:T(128)}, f32[8,64,512]{2,1,0:T(8,128)S(1)}, s32[2]{0:T(128)S(1)}, bf16[2,64,4096]{2,1,0:T(8,128)(2,1)}, s32[2]{0:T(128)S(1)}, /*index=5*/bf1...) while((s32[]{:T(128)}, f32[8,64,512]{2,1,0:T(8,128)S(1)}, ...), condition=%wide.region_2.4_spmd, body=%wide.region_0.3_spmd.sunk | while | flops 272662528 | bytes 4063449 | solution.py:64
  91.9 0.6 dynamic_slice.71
  94.2 1.1 constant_dynamic-slice_fusion.2
  95.3 1.1 dot_general.7
  96.4 1.2 multiply_reduce_fusion.2
  97.6 0.6 dynamic_slice.70
  100.0 0.6 dynamic_slice.71
  102.2 1.1 constant_dynamic-slice_fusion.2
  103.3 1.1 dot_general.7
  104.5 1.2 multiply_reduce_fusion.2
  105.7 0.6 dynamic_slice.70
  108.0 0.9 convert_element_type.18
  108.9 0.0 reduce-scatter.2.cloned.1.call-update
  108.9 30.6 %reduce-scatter.2.cloned.1.call-done = bf16[64,512]{1,0:T(8,128)(2,1)} async-done(((bf16[512,512]{1,0:T(8,128)(2,1)}), bf16[64,512]{1,0:T(8,128)(2,1)}) %reduce-scatter.2.cloned.1.call-update) | async-done | bytes 65552 | tf_op jit(solution)/shard_map/reduce_scatter | solution.py:68
  139.5 1.5 %convert_element_type.20 = f32[64,512]{1,0:T(8,128)} convert(bf16[64,512]{1,0:T(8,128)(2,1)} %reduce-scatter.2.cloned.1.call-done) | non-fusion elementwise | flops 32768 | bytes 196608 | tf_op jit(solution)/shard_map/convert_element_type | solution.py:73
  (17 shorter events, 0.2 us)
Async XLA Ops:
  6.5 50.3 %copy-start = (bf16[256,1,512]{2,0,1:T(8,128)(2,1)S(1)}, bf16[256,1,512]{2,0,1:T(8,128)(2,1)}, u32[]{:S(2)}) copy-start(bf16[256,1,512]{2,0,1:T(8,128)(2,1)} %param.18) | copy-start | bytes 786436
  6.5 5.9 %copy-start.2 = (s32[1,2]{1,0:T(1,128)S(1)}, s32[1,2]{1,0:T(1,128)}, u32[]{:S(2)}) copy-start(s32[1,2]{1,0:T(1,128)} %param.15) | copy-start | bytes 28
  6.5 6.0 %copy-start.3 = (s32[1,2]{1,0:T(1,128)S(1)}, s32[1,2]{1,0:T(1,128)}, u32[]{:S(2)}) copy-start(s32[1,2]{1,0:T(1,128)} %param.14) | copy-start | bytes 28
  6.5 37.9 %copy-start.1 = (bf16[64,1,512]{2,0,1:T(8,128)(2,1)S(1)}, bf16[64,1,512]{2,0,1:T(8,128)(2,1)}, u32[]{:S(2)}) copy-start(bf16[64,1,512]{2,0,1:T(8,128)(2,1)} %param.19) | copy-start | bytes 196612
  46.2 24.7 %all-to-all-start = ((bf16[2,64,1,512]{3,0,2,1:T(2,128)(2,1)}), bf16[2,64,1,512]{3,0,2,1:T(2,128)(2,1)S(1)}, u32[]{:S(2)}, u32[]{:S(2)}) async-start(bf16[2,64,1,512]{3,0,2,1:T(2,128)(2,1)} %broadcast_select_fusion.1), calls=%async_computation | async-start | bytes 262144 | tf_op jit(solution)/shard_map/all_to_all | solution.py:43
  57.7 34.2 %copy-start.4 = (s32[1,2]{1,0:T(1,128)S(1)}, s32[1,2]{1,0:T(1,128)}, u32[]{:S(2)}) copy-start(s32[1,2]{1,0:T(1,128)} %param.13) | copy-start | bytes 28
  70.8 20.9 %all-to-all-start.1 = ((bf16[2,64,1,512]{3,0,2,1:T(2,128)(2,1)}), bf16[2,64,1,512]{3,0,2,1:T(2,128)(2,1)S(1)}, u32[]{:S(2)}, u32[]{:S(2)}) async-start(bf16[2,64,1,512]{3,0,2,1:T(2,128)(2,1)} %broadcast_select_fusion), calls=%async_computation.1 | async-start | bytes 262144 | tf_op jit(solution)/shard_map/all_to_all | solution.py:40
  77.2 62.3 %reduce-scatter.2.cloned.1.call-start = ((), (), s32[]{:S(2)}) async-start(), calls=%async_computation.3 | async-start | bytes 589824 | tf_op jit(solution)/shard_map/reduce_scatter | solution.py:68
Sparse Core Ops, SparseCore 0:
  109.0 30.4 reduce-scatter.1
where the time goes:
time: 148 us
  waiting for transfers between devices  57.4 us (39%)
  blocking collectives  31.5 us (21%)
  starting transfers between devices  16.7 us (11%)
  between operations  14.2 us (10%)
  local copies, waits for them, and re-layouts  13 us (9%)
  loops' own time  6.83 us (5%)
  other arithmetic  5.82 us (4%)
  matrix products  2.48 us (2%)
    unnamed x1, blocking collectives  31.5 us
    reduce_scatter x1, waiting for transfers between devices, per_device(): lax.psum_scatter(rounded.reshape(groups * inner, rank).astype(jnp.bfloat1...  30.6 us
    all_to_all x1, waiting for transfers between devices, per_device(): lax.all_to_all(outgoing(asked_two, factor_b, count), 'tiles', split_axis=...  14.5 us
    all_to_all x1, waiting for transfers between devices, per_device(): lax.all_to_all(outgoing(asked_three, factor_c, count), 'tiles', split_axi...  12.3 us
    all_to_all x1, starting transfers between devices, per_device(): lax.all_to_all(outgoing(asked_three, factor_c, count), 'tiles', split_axi...  10.3 us
    another operation x1, loops' own time, per_device(): lax.fori_loop(0, count, accumulate, jnp.zeros((groups, inner, rank), jnp....  6.83 us
    all_to_all x1, starting transfers between devices, per_device(): lax.all_to_all(outgoing(asked_two, factor_b, count), 'tiles', split_axis=...  6.3 us
  transfers between devices with their start and end apart: 3, of which 3 were waited for; matrix products, arithmetic and copies ran while one was open for 1% of the time, Pallas kernels for 0%

commit v1 on v0

--- a/solution.py
+++ b/solution.py
@@ -40,8 +40,18 @@
         lax.all_to_all(
             outgoing(asked_two, factor_b, count), "tiles", split_axis=1, concat_axis=2, tiled=True
         ),
-        lax.all_to_all(
-            outgoing(asked_three, factor_c, count), "tiles", split_axis=1, concat_axis=2, tiled=True
+        jnp.concatenate(
+            lax.all_to_all(
+                jnp.stack(
+                    jnp.split(
+                        outgoing(asked_three, factor_c, count), lax.axis_size("tiles"), axis=1
+                    )
+                ),
+                "tiles",
+                0,
+                0,
+            ),
+            axis=2,
         ),
     )
     pick_two = jnp.arange(count, dtype=jnp.int32)

time: 148 us -> 187 us (1.26)
  the two profiles are of different devices: /device:TPU:4 before, /device:TPU:6 now
where the time goes in v1:
time: 187 us
  waiting for transfers between devices  57.7 us (31%)
  local copies, waits for them, and re-layouts  50.6 us (27%)
  blocking collectives  32.4 us (17%)
  starting transfers between devices  15.7 us (8%)
  between operations  14.2 us (8%)
  loops' own time  8.39 us (4%)
  other arithmetic  5.16 us (3%)
  matrix products  2.5 us (1%)
    unnamed x76, local copies, waits for them, and re-layouts  37.9 us
    unnamed x1, blocking collectives  32.4 us
    reduce_scatter x1, waiting for transfers between devices, per_device(): lax.psum_scatter(rounded.reshape(groups * inner, rank).astype(jnp.bfloat1...  30.6 us
    all_to_all x1, waiting for transfers between devices, per_device(): lax.all_to_all(outgoing(asked_two, factor_b, count), 'tiles', split_axis=...  14.5 us
    all_to_all x1, waiting for transfers between devices, per_device(): lax.all_to_all(jnp.stack(jnp.split(outgoing(asked_three, factor_c, count)...  12.6 us
    all_to_all x1, starting transfers between devices, per_device(): lax.all_to_all(jnp.stack(jnp.split(outgoing(asked_three, factor_c, count)...  9.39 us
    another operation x1, loops' own time, per_device(): lax.fori_loop(0, count, accumulate, jnp.zeros((groups, inner, rank), jnp....  8.39 us
    all_to_all x1, starting transfers between devices, per_device(): lax.all_to_all(outgoing(asked_two, factor_b, count), 'tiles', split_axis=...  6.29 us
  transfers between devices with their start and end apart: 3, of which 3 were waited for; matrix products, arithmetic and copies ran while one was open for 1% of the time, Pallas kernels for 0%

profile of v1, /device:TPU:6, one launch (start us, length us, event | category | flops | bytes accessed | tf_op | source)
XLA Modules:
  0.0 186.6 jit_solution(441126362347631427)
XLA Ops:
  6.5 0.7 compare_select_fusion.3
  7.3 0.7 compare_select_fusion.2
  7.9 1.3 dynamic-slice
  9.9 1.3 gather_fusion.2
  11.2 1.3 gather_fusion.3
  12.6 32.4 %all-reduce.2 = (s32[128]{0:T(128)S(1)}, s32[128]{0:T(128)S(1)}) all-reduce(s32[128]{0:T(128)S(1)} %fusion.4, s32[128]{0:T(128)S(1)} %fusion.5), channel_id=1, replica_groups=mesh['blk'=8,'tiles'=64] {'tiles'}, use_global_device_ids=true, to_apply=%add | all-reduce | flops 256 | bytes 2048
  45.7 0.9 gather_fusion
  46.7 0.6 constant_dynamic-update-slice_fusion.63
  47.3 0.6 constant_dynamic-update-slice_fusion.62
  47.9 0.6 constant_dynamic-update-slice_fusion.61
  48.5 0.6 constant_dynamic-update-slice_fusion.60
  53.1 0.6 constant_dynamic-update-slice_fusion.52
  53.7 0.6 constant_dynamic-update-slice_fusion.51
  54.3 0.6 constant_dynamic-update-slice_fusion.50
  54.9 0.6 constant_dynamic-update-slice_fusion.49
  55.5 0.6 constant_dynamic-update-slice_fusion.48
  56.0 0.6 constant_dynamic-update-slice_fusion.47
  56.6 0.6 constant_dynamic-update-slice_fusion.46
  57.2 0.6 constant_dynamic-update-slice_fusion.45
  57.8 0.6 constant_dynamic-update-slice_fusion.44
  58.4 0.6 constant_dynamic-update-slice_fusion.43
  59.0 0.6 constant_dynamic-update-slice_fusion.42
  59.5 0.6 constant_dynamic-update-slice_fusion.41
  64.2 0.6 constant_dynamic-update-slice_fusion.33
  64.8 0.6 constant_dynamic-update-slice_fusion.32
  65.3 0.6 constant_dynamic-update-slice_fusion.31
  65.9 0.6 constant_dynamic-update-slice_fusion.30
  66.5 0.6 constant_dynamic-update-slice_fusion.29
  67.1 0.6 constant_dynamic-update-slice_fusion.28
  67.7 0.6 constant_dynamic-update-slice_fusion.27
  68.3 0.6 constant_dynamic-update-slice_fusion.26
  68.8 0.6 constant_dynamic-update-slice_fusion.25
  69.4 0.6 constant_dynamic-update-slice_fusion.24
  70.0 0.6 constant_dynamic-update-slice_fusion.23
  70.6 0.6 constant_dynamic-update-slice_fusion.22
  75.2 0.6 constant_dynamic-update-slice_fusion.14
  75.8 0.6 constant_dynamic-update-slice_fusion.13
  76.4 0.6 constant_dynamic-update-slice_fusion.12
  77.0 0.6 constant_dynamic-update-slice_fusion.11
  77.6 0.6 constant_dynamic-update-slice_fusion.10
  78.1 0.6 constant_dynamic-update-slice_fusion.9
  78.7 0.6 constant_dynamic-update-slice_fusion.8
  79.3 0.6 constant_dynamic-update-slice_fusion.7
  79.9 0.6 constant_dynamic-update-slice_fusion.6
  84.0 9.4 %all-to-all-start = ((bf16[64,2,1,1,512]{4,1,3,2,0:T(2,128)(2,1)}), bf16[64,2,1,1,512]{4,1,3,2,0:T(2,128)(2,1)S(1)}, u32[]{:S(2)}, u32[]{:S(2)}) async-start(bf16[64,2,1,1,512]{4,1,3,2,0:T(2,128)(2,1)} %constant_dynamic-update-slice_fusion), calls=%async_computation | async-start | bytes 262144 | tf_op jit(solution)/shard_map/all_to_all | solution.py:44
  93.4 0.8 gather_fusion.1
  94.2 0.9 broadcast_select_fusion
  95.1 12.6 %all-to-all-done = bf16[64,2,1,1,512]{4,1,3,2,0:T(2,128)(2,1)S(1)} async-done(((bf16[64,2,1,1,512]{4,1,3,2,0:T(2,128)(2,1)}), bf16[64,2,1,1,512]{4,1,3,2,0:T(2,128)(2,1)S(1)}, u32[]{:S(2)}, u32[]{:S(2)}) %all-to-all-start) | async-done | bytes 131104 | tf_op jit(solution)/shard_map/all_to_all | solution.py:44
  107.7 6.3 %all-to-all-start.1 = ((bf16[2,64,1,512]{3,0,2,1:T(2,128)(2,1)}), bf16[2,64,1,512]{3,0,2,1:T(2,128)(2,1)S(1)}, u32[]{:S(2)}, u32[]{:S(2)}) async-start(bf16[2,64,1,512]{3,0,2,1:T(2,128)(2,1)} %broadcast_select_fusion), calls=%async_computation.1 | async-start | bytes 262144 | tf_op jit(solution)/shard_map/all_to_all | solution.py:40
  114.1 14.5 %all-to-all-done.1 = bf16[2,64,1,512]{3,0,2,1:T(2,128)(2,1)S(1)} async-done(((bf16[2,64,1,512]{3,0,2,1:T(2,128)(2,1)}), bf16[2,64,1,512]{3,0,2,1:T(2,128)(2,1)S(1)}, u32[]{:S(2)}, u32[]{:S(2)}) %all-to-all-start.1) | async-done | bytes 131104 | tf_op jit(solution)/shard_map/all_to_all | solution.py:40
  128.7 18.1 %while.14 = (s32[]{:T(128)}, f32[8,64,512]{2,1,0:T(8,128)S(1)}, s32[2]{0:T(128)S(1)}, bf16[2,64,4096]{2,1,0:T(8,128)(2,1)}, s32[2]{0:T(128)S(1)}, /*index=5*/bf1...) while((s32[]{:T(128)}, f32[8,64,512]{2,1,0:T(8,128)S(1)}, ...), condition=%wide.region_2.4_spmd, body=%wide.region_0.3_spmd.sunk | while | flops 272662528 | bytes 4063449 | solution.py:74
  128.7 0.7 dynamic_slice.71
  131.5 1.1 constant_dynamic-slice_fusion.2
  132.6 1.1 dot_general.7
  133.7 1.2 multiply_reduce_fusion.2
  135.0 0.7 dynamic_slice.70
  137.8 0.7 dynamic_slice.71
  140.5 1.1 constant_dynamic-slice_fusion.2
  141.6 1.1 dot_general.7
  142.7 1.3 multiply_reduce_fusion.2
  144.0 0.7 dynamic_slice.70
  146.8 0.9 convert_element_type.18
  147.7 30.6 %reduce-scatter.2.cloned.1.call-done = bf16[64,512]{1,0:T(8,128)(2,1)} async-done(((bf16[512,512]{1,0:T(8,128)(2,1)}), bf16[64,512]{1,0:T(8,128)(2,1)}) %reduce-scatter.2.cloned.1.call-update) | async-done | bytes 65552 | tf_op jit(solution)/shard_map/reduce_scatter | solution.py:78
  178.3 1.5 convert_element_type.20
  (65 shorter events, 17.0 us)
Async XLA Ops:
  6.5 86.8 %copy-start = (bf16[256,1,512]{2,0,1:T(8,128)(2,1)S(1)}, bf16[256,1,512]{2,0,1:T(8,128)(2,1)}, u32[]{:S(2)}) copy-start(bf16[256,1,512]{2,0,1:T(8,128)(2,1)} %param.18) | copy-start | bytes 786436
  6.5 5.9 %copy-start.2 = (s32[1,2]{1,0:T(1,128)S(1)}, s32[1,2]{1,0:T(1,128)}, u32[]{:S(2)}) copy-start(s32[1,2]{1,0:T(1,128)} %param.15) | copy-start | bytes 28
  6.5 6.0 %copy-start.3 = (s32[1,2]{1,0:T(1,128)S(1)}, s32[1,2]{1,0:T(1,128)}, u32[]{:S(2)}) copy-start(s32[1,2]{1,0:T(1,128)} %param.14) | copy-start | bytes 28
  6.5 39.1 %copy-start.1 = (bf16[64,1,512]{2,0,1:T(8,128)(2,1)S(1)}, bf16[64,1,512]{2,0,1:T(8,128)(2,1)}, u32[]{:S(2)}) copy-start(bf16[64,1,512]{2,0,1:T(8,128)(2,1)} %param.19) | copy-start | bytes 196612
  84.0 23.8 %all-to-all-start = ((bf16[64,2,1,1,512]{4,1,3,2,0:T(2,128)(2,1)}), bf16[64,2,1,1,512]{4,1,3,2,0:T(2,128)(2,1)S(1)}, u32[]{:S(2)}, u32[]{:S(2)}) async-start(bf16[64,2,1,1,512]{4,1,3,2,0:T(2,128)(2,1)} %constant_dynamic-update-slice_fusion), calls=%async_computation | async-start | bytes 262144 | tf_op jit(solution)/shard_map/all_to_all | solution.py:44
  94.2 34.5 %copy-start.4 = (s32[1,2]{1,0:T(1,128)S(1)}, s32[1,2]{1,0:T(1,128)}, u32[]{:S(2)}) copy-start(s32[1,2]{1,0:T(1,128)} %param.13) | copy-start | bytes 28
  107.7 20.8 %all-to-all-start.1 = ((bf16[2,64,1,512]{3,0,2,1:T(2,128)(2,1)}), bf16[2,64,1,512]{3,0,2,1:T(2,128)(2,1)S(1)}, u32[]{:S(2)}, u32[]{:S(2)}) async-start(bf16[2,64,1,512]{3,0,2,1:T(2,128)(2,1)} %broadcast_select_fusion), calls=%async_computation.1 | async-start | bytes 262144 | tf_op jit(solution)/shard_map/all_to_all | solution.py:40
  114.0 64.3 %reduce-scatter.2.cloned.1.call-start = ((), (), s32[]{:S(2)}) async-start(), calls=%async_computation.3 | async-start | bytes 589824 | tf_op jit(solution)/shard_map/reduce_scatter | solution.py:78
Sparse Core Ops, SparseCore 0:
  147.8 30.4 reduce-scatter.1
